TPU v7x, 256 devices: a whole 4x4x8 slice. The times are simulated.
256 devices in a mesh: wave: 8 (over z_hi, core), brick: 32 (over z_lo, x, y).
Axes of the slice: x: 4, y: 4, z: 8 (z_hi: 4, z_lo: 2; z = z_hi * 2 + z_lo), core: 2. Of those that a mesh axis runs over, the one named last changes fastest.
Arguments:
- sources: float32 [8, 6, 256, 6, 4096], P('wave', None, 'brick'), may hold values from -6 to 6
- permittivity: float32 [256, 6, 4096], P('brick'), may hold values from 1 to 4
- wave_number_sq: float32 [8], P('wave'), may hold values from 0.5 to 3
- pixel_list: int32 [32, 256], P('brick'), may hold values from 0 to 255, each once within a row
Outputs:
- design_grad: float32 [32, 32768], P('brick')
Inputs may be any that keep to these rules, and one draw needn't show every extreme that they name: `pixel_list`: each row is a permutation of 0 to 255.
All inputs are finite; a program needn't handle non-finite values.
Results may differ from a plain program's by a relative error of at most 0.0001.
Values sent between devices are 32-bit elements; how exact they have to be, the bound alone decides.
A program may use at most 128 MiB of HBM per device.

v0:
```python
import jax
import jax.numpy as jnp
from jax import lax
from jax.sharding import PartitionSpec as P

SWEEPS = 3
RADIUS = 2
RUN = 128
RELAX = 0.5


def padded_2(x, sides, width):
    for axis, dim in sides:
        peers, length = (lax.axis_size(axis), x.shape[dim])
        up = [(i, (i + 1) % peers) for i in range(peers - 1)]
        down = [(j, i) for i, j in up]
        last = lax.slice_in_dim(x, length - width, length, axis=dim)
        initial = lax.slice_in_dim(x, 0, width, axis=dim)
        before = lax.ppermute(last, axis, up)
        after = lax.ppermute(initial, axis, down)
        x = jnp.concatenate([before, x, after], axis=dim)
    return x


def ahead_x(values):
    return values[..., 1:, :, :] - values[..., :-1, :, :]


def ahead_y(values):
    return jnp.concatenate([values[..., 1:], jnp.zeros_like(values[..., :1])], -1) - values


def ahead_z(values):
    return jnp.concatenate([values[..., 1:, :], jnp.zeros_like(values[..., :1, :])], -2) - values


def behind_y(values):
    return values - jnp.concatenate([jnp.zeros_like(values[..., :1]), values[..., :-1]], -1)


def behind_z(values):
    return values - jnp.concatenate([jnp.zeros_like(values[..., :1, :]), values[..., :-1, :]], -2)


def curl_curl(padded):
    comp_x = padded[..., 0, :, :, :]
    comp_y = padded[..., 1, :, :, :]
    comp_z = padded[..., 2, :, :, :]
    lead_x = comp_x[..., :-1, :, :]
    lead_y = comp_y[..., :-1, :, :]
    lead_z = comp_z[..., :-1, :, :]
    mag_x = ahead_y(lead_z) - ahead_z(lead_y)
    mag_y = ahead_z(lead_x) - ahead_x(comp_z)
    mag_z = ahead_x(comp_y) - ahead_y(lead_x)
    curl_x = behind_y(mag_z[..., 1:, :, :]) - behind_z(mag_y[..., 1:, :, :])
    curl_y = behind_z(mag_x[..., 1:, :, :]) - ahead_x(mag_z)
    curl_z = ahead_x(mag_y) - behind_y(mag_x[..., 1:, :, :])
    return jnp.stack([curl_x, curl_y, curl_z], -4)


def relax_step(fields, padded, drive_all, permit, wave_sq, diagonal):
    return fields + RELAX * (drive_all - curl_curl(padded) - wave_sq * permit * fields) / diagonal


def smooth_padded(padded, length, along):
    summed = jnp.zeros_like(lax.slice_in_dim(padded, 0, length, axis=along))
    for offset in range(2 * RADIUS + 1):
        weight = (RADIUS + 1 - abs(offset - RADIUS)) / (RADIUS + 1) ** 2
        summed = summed + weight * lax.slice_in_dim(padded, offset, offset + length, axis=along)
    return summed


def pick_runs(smooth, order):
    blocks = smooth.reshape(-1, RUN)
    return jnp.take(blocks, order, axis=0).reshape(1, -1)


def on_device(sources, permittivity, wave_number_sq, pixel_list):
    wave_sq = wave_number_sq[0]
    brick_rows = permittivity.shape[0]
    layers = permittivity.shape[1]
    columns = permittivity.shape[2]
    drive_all = sources[0].reshape(2, 3, brick_rows, layers, columns)
    diagonal = 4.0 + wave_sq * permittivity
    fields = RELAX * drive_all / diagonal
    for sweep_index in range(SWEEPS - 1):
        padded = padded_2(fields, (("brick", 2),), 1)
        fields = relax_step(fields, padded, drive_all, permittivity, wave_sq, diagonal)
    density = -wave_sq * jnp.sum(fields[0] * fields[1], axis=(0, 2))
    row_sum = lax.psum(density, "wave")
    along_y = smooth_padded(jnp.pad(row_sum, ((0, 0), (RADIUS, RADIUS))), columns, 1)
    widened_rows = padded_2(along_y, (("brick", 0),), RADIUS)
    smooth = smooth_padded(widened_rows, brick_rows, 0)
    return pick_runs(smooth, pixel_list[0])


def solution(mesh):
    return jax.shard_map(
        on_device,
        mesh=mesh,
        in_specs=(
            P("wave", None, "brick", None, None),
            P("brick", None, None),
            P("wave"),
            P("brick", None),
        ),
        out_specs=P("brick", None),
        check_vma=False,
    )
```

profile of v0, /device:TPU:30, one launch (start us, length us, event | category | flops | bytes accessed | tf_op | source)
XLA Modules:
  0.0 236.2 jit_solution(8491026144020708894)
XLA Ops:
  10.3 3.0 %multiply_divide_fusion = f32[2,3,8,6,4096]{4,2,3,1,0:T(8,128)S(1)} fusion(f32[2,3,8,6,4096]{4,2,3,1,0:T(8,128)} %bitcast.41, f32[8,6,4096]{2,0,1:T(8,128)S(1)} %get-tuple-element.5), kind=kLoop, calls=%fused_computation.14 | loop fusion | flops 2359296 | bytes 10223616 | tf_op jit(solution)/shard_map/div | solution.py:85
  14.5 3.4 %collective-permute-start = (f32[2,3,1,6,4096]{4,2,3,1,0:T(1,128)S(1)}, f32[2,3,1,6,4096]{4,2,3,1,0:T(1,128)S(1)}, u32[]{:S(2)}, u32[]{:S(2)}) collective-permute-start(f32[2,3,1,6,4096]{4,2,3,1,0:T(1,128)S(1)} %get-tuple-element.15), channel_id=1, source_target_pairs={{0,1},{1,2},{2,3},{3,4},{4,5},{5,6},{6,7},{7,8},{8,9},{9,10},{10,1... | collective-permute-start | bytes 1769480 | tf_op jit(solution)/shard_map/ppermute | solution.py:19
  17.9 2.4 %collective-permute-start.1 = (f32[2,3,1,6,4096]{4,2,3,1,0:T(1,128)S(1)}, f32[2,3,1,6,4096]{4,2,3,1,0:T(1,128)S(1)}, u32[]{:S(2)}, u32[]{:S(2)}) collective-permute-start(f32[2,3,1,6,4096]{4,2,3,1,0:T(1,128)S(1)} %get-tuple-element.16), channel_id=1, source_target_pairs={{1,0},{2,1},{3,2},{4,3},{5,4},{6,5},{7,6},{8,7},{9,8},{10,9},{11,1... | collective-permute-start | bytes 1769480 | tf_op jit(solution)/shard_map/ppermute | solution.py:20
  20.3 11.1 %collective-permute-done = f32[2,3,1,6,4096]{4,2,3,1,0:T(1,128)S(1)} collective-permute-done((f32[2,3,1,6,4096]{4,2,3,1,0:T(1,128)S(1)}, f32[2,3,1,6,4096]{4,2,3,1,0:T(1,128)S(1)}, u32[]{:S(2)}, u32[]{:S(2)}) %collective-permute-start) | collective-permute-done | bytes 589856 | tf_op jit(solution)/shard_map/ppermute | solution.py:19
  31.4 7.3 %collective-permute-done.1 = f32[2,3,1,6,4096]{4,2,3,1,0:T(1,128)S(1)} collective-permute-done((f32[2,3,1,6,4096]{4,2,3,1,0:T(1,128)S(1)}, f32[2,3,1,6,4096]{4,2,3,1,0:T(1,128)S(1)}, u32[]{:S(2)}, u32[]{:S(2)}) %collective-permute-start.1) | collective-permute-done | bytes 589856 | tf_op jit(solution)/shard_map/ppermute | solution.py:20
  44.3 2.6 %slice.281 = f32[2,9,6,4095]{3,1,2,0:T(8,128)} slice(f32[2,10,6,4096]{3,1,2,0:T(8,128)S(1)} %get-tuple-element.11), slice={[0:2], [0:9], [0:6], [1:4096]} | slice | bytes 3538080 | tf_op jit(solution)/shard_map/slice | solution.py:30
  48.6 5.7 %fusion.10 = (f32[2,9,6,4096]{3,1,2,0:T(8,128)S(1)}, f32[2,9,6,4096]{3,1,2,0:T(8,128)}, f32[2,9,6,4096]{3,1,2,0:T(8,128)S(1)}) fusion(f32[2,10,6,4096]{3,1,2,0:T(8,128)S(1)} %get-tuple-element.10, f32[2,9,6,4095]{3,1,2,0:T(8,128)S(1)} %slice.271, f32[2,10,6,4096]{3,1,2,0:T(8,128)S(1)} %get-tuple-element.12, f32[2,10,6,4096]{3,1,2,0:T(8,128)S(1)} %get-tuple-element.11, ...), kind=kLoop, calls=%fused_computation.27 | loop fusion | flops 3981312 | bytes 20642976 | tf_op jit(solution)/shard_map/sub | solution.py:54
  58.4 3.1 %slice.280 = f32[2,8,5,4096]{3,1,2,0:T(8,128)} slice(f32[2,9,6,4096]{3,1,2,0:T(8,128)} %get-tuple-element.27), slice={[0:2], [1:9], [0:5], [0:4096]} | slice | bytes 2621440 | tf_op jit(solution)/shard_map/slice | solution.py:42
  61.5 8.6 %subtract_bitcast_fusion.1 = (f32[2,1,8,6,4096]{4,2,3,0,1:T(8,128)S(1)}, f32[2,1,8,6,4096]{4,2,3,0,1:T(8,128)}, f32[2,1,8,6,4096]{4,2,3,0,1:T(8,128)}) fusion(f32[2,8,5,4096]{3,1,2,0:T(8,128)} %slice.280, f32[2,8,6,4095]{3,1,2,0:T(8,128)} %slice.274, f32[2,9,6,4096]{3,1,2,0:T(8,128)} %get-tuple-element.27, f32[2,9,6,4096]{3,1,2,0:T(8,128)S(1)} %get-tuple-element.26, ...), kind=kLoop, calls=%fused_computation.46 | loop fusion | flops 3538944 | bytes 18349312 | tf_op jit(solution)/shard_map/stack | solution.py:58
  70.2 4.3 %fusion.6 = f32[2,3,8,6,4096]{4,2,3,1,0:T(8,128)S(1)} fusion(f32[8,6,4096]{2,0,1:T(8,128)} %get-tuple-element.6, f32[8,6,4096]{2,0,1:T(8,128)} %copy-done.5, f32[2,3,8,6,4096]{4,2,3,1,0:T(8,128)S(1)} %bitcast.44, f32[2,1,8,6,4096]{4,2,3,0,1:T(8,128)} %get-tuple-element.25, f32[2,1,8,6,4096]{4,2,3,0,1:T(8,128)} %get-tuple-element.24, ...), kind=kLoop, calls=%fused_computation.13 | loop fusion | flops 11796480 | bytes 15728640 | tf_op jit(solution)/shard_map/add | solution.py:62
  74.5 2.2 copy-done
  79.9 4.1 %collective-permute-start.3 = (f32[2,3,1,6,4096]{4,2,3,1,0:T(1,128)S(1)}, f32[2,3,1,6,4096]{4,2,3,1,0:T(1,128)}, u32[]{:S(2)}, u32[]{:S(2)}) collective-permute-start(f32[2,3,1,6,4096]{4,2,3,1,0:T(1,128)S(1)} %get-tuple-element.14), channel_id=1, source_target_pairs={{1,0},{2,1},{3,2},{4,3},{5,4},{6,5},{7,6},{8,7},{9,8},{10,9},{11,1... | collective-permute-start | bytes 1769480 | tf_op jit(solution)/shard_map/ppermute | solution.py:20
  84.0 9.7 %collective-permute-done.2 = f32[2,3,1,6,4096]{4,2,3,1,0:T(1,128)S(1)} collective-permute-done((f32[2,3,1,6,4096]{4,2,3,1,0:T(1,128)S(1)}, f32[2,3,1,6,4096]{4,2,3,1,0:T(1,128)S(1)}, u32[]{:S(2)}, u32[]{:S(2)}) %collective-permute-start.2) | collective-permute-done | bytes 589856 | tf_op jit(solution)/shard_map/ppermute | solution.py:19
  94.5 5.4 %collective-permute-done.3 = f32[2,3,1,6,4096]{4,2,3,1,0:T(1,128)} collective-permute-done((f32[2,3,1,6,4096]{4,2,3,1,0:T(1,128)S(1)}, f32[2,3,1,6,4096]{4,2,3,1,0:T(1,128)}, u32[]{:S(2)}, u32[]{:S(2)}) %collective-permute-start.3) | collective-permute-done | bytes 589856 | tf_op jit(solution)/shard_map/ppermute | solution.py:20
  100.0 3.5 %pad_maximum_fusion.1 = f32[2,3,10,6,4096]{4,2,3,1,0:T(8,128)S(1)} fusion(f32[2,3,1,6,4096]{4,2,3,1,0:T(1,128)} %collective-permute-done.3, f32[2,3,8,6,4096]{4,2,3,1,0:T(8,128)} %copy-done, f32[2,3,1,6,4096]{4,2,3,1,0:T(1,128)} %copy-done.6), kind=kLoop, calls=%fused_computation.2 | loop fusion | flops 2949120 | bytes 11796480 | tf_op jit(solution)/shard_map/concatenate | solution.py:21
  107.2 2.6 %slice.304 = f32[2,9,6,4095]{3,1,2,0:T(8,128)} slice(f32[2,10,6,4096]{3,1,2,0:T(8,128)S(1)} %get-tuple-element.8), slice={[0:2], [0:9], [0:6], [1:4096]} | slice | bytes 3538080 | tf_op jit(solution)/shard_map/slice | solution.py:30
  111.4 5.7 %fusion.8 = (f32[2,9,6,4096]{3,1,2,0:T(8,128)S(1)}, f32[2,9,6,4096]{3,1,2,0:T(8,128)}, f32[2,9,6,4096]{3,1,2,0:T(8,128)S(1)}) fusion(f32[2,10,6,4096]{3,1,2,0:T(8,128)S(1)} %get-tuple-element.7, f32[2,9,6,4095]{3,1,2,0:T(8,128)S(1)} %slice.294, f32[2,10,6,4096]{3,1,2,0:T(8,128)S(1)} %get-tuple-element.9, f32[2,10,6,4096]{3,1,2,0:T(8,128)S(1)} %get-tuple-element.8, ...), kind=kLoop, calls=%fused_computation.20 | loop fusion | flops 3981312 | bytes 20642976 | tf_op jit(solution)/shard_map/sub | solution.py:54
  121.3 3.1 %slice.303 = f32[2,8,5,4096]{3,1,2,0:T(8,128)} slice(f32[2,9,6,4096]{3,1,2,0:T(8,128)} %get-tuple-element.21), slice={[0:2], [1:9], [0:5], [0:4096]} | slice | bytes 2621440 | tf_op jit(solution)/shard_map/slice | solution.py:42
  124.4 9.2 %subtract_bitcast_fusion = (f32[2,1,8,6,4096]{4,2,3,0,1:T(8,128)}, f32[2,1,8,6,4096]{4,2,3,0,1:T(8,128)}, f32[2,1,8,6,4096]{4,2,3,0,1:T(8,128)}) fusion(f32[2,8,5,4096]{3,1,2,0:T(8,128)} %slice.303, f32[2,8,6,4095]{3,1,2,0:T(8,128)} %slice.297, f32[2,9,6,4096]{3,1,2,0:T(8,128)} %get-tuple-element.21, f32[2,9,6,4096]{3,1,2,0:T(8,128)S(1)} %get-tuple-element.20, ...), kind=kLoop, calls=%fused_computation.45 | loop fusion | flops 3538944 | bytes 18349312 | tf_op jit(solution)/shard_map/stack | solution.py:58
  133.7 5.5 %fusion.3 = f32[2,3,8,6,4096]{4,2,3,1,0:T(8,128)S(1)} fusion(f32[2,3,8,6,4096]{4,2,3,1,0:T(8,128)S(1)} %bitcast.47, f32[8,6,4096]{2,0,1:T(8,128)} %get-tuple-element.6, f32[8,6,4096]{2,0,1:T(8,128)} %copy-done.5, f32[2,1,8,6,4096]{4,2,3,0,1:T(8,128)} %get-tuple-element.19, f32[2,1,8,6,4096]{4,2,3,0,1:T(8,128)} %get-tuple-element.18, ...), kind=kLoop, calls=%fused_computation.9 | loop fusion | flops 21233664 | bytes 20447232 | tf_op jit(solution)/shard_map/add | solution.py:62
  140.1 73.5 %all-reduce.19.cloned.1.call-done = f32[8,4096]{1,0:T(8,128)} async-done(((f32[8,4096]{1,0:T(8,128)}), f32[8,4096]{1,0:T(8,128)}) %all-reduce.19.cloned.1.call-update) | async-done | bytes 131088 | tf_op jit(solution)/shard_map/psum | solution.py:90
  215.2 2.5 %collective-permute-start.4 = (f32[2,4096]{1,0:T(2,128)S(1)}, f32[2,4096]{1,0:T(2,128)S(1)}, u32[]{:S(2)}, u32[]{:S(2)}) collective-permute-start(f32[2,4096]{1,0:T(2,128)S(1)} %get-tuple-element.29), channel_id=1, source_target_pairs={{0,1},{1,2},{2,3},{3,4},{4,5},{5,6},{6,7},{7,8},{8,9},{9,10},{10,1... | collective-permute-start | bytes 98312 | tf_op jit(solution)/shard_map/ppermute | solution.py:19
  217.7 3.4 %collective-permute-start.5 = (f32[2,4096]{1,0:T(2,128)S(1)}, f32[2,4096]{1,0:T(2,128)S(1)}, u32[]{:S(2)}, u32[]{:S(2)}) collective-permute-start(f32[2,4096]{1,0:T(2,128)S(1)} %get-tuple-element.30), channel_id=1, source_target_pairs={{1,0},{2,1},{3,2},{4,3},{5,4},{6,5},{7,6},{8,7},{9,8},{10,9},{11,1... | collective-permute-start | bytes 98312 | tf_op jit(solution)/shard_map/ppermute | solution.py:20
  221.1 6.6 %collective-permute-done.5 = f32[2,4096]{1,0:T(2,128)S(1)} collective-permute-done((f32[2,4096]{1,0:T(2,128)S(1)}, f32[2,4096]{1,0:T(2,128)S(1)}, u32[]{:S(2)}, u32[]{:S(2)}) %collective-permute-start.5) | collective-permute-done | bytes 32800 | tf_op jit(solution)/shard_map/ppermute | solution.py:20
  (58 shorter events, 33.2 us)
Async XLA Ops:
  6.5 207.1 %all-reduce.19.cloned.1.call-start = ((), (), s32[]{:S(2)}) async-start(), calls=%async_computation | async-start | bytes 262144 | tf_op jit(solution)/shard_map/psum | solution.py:90
  9.3 0.9 copy-start.5
  14.5 17.0 %collective-permute-start = (f32[2,3,1,6,4096]{4,2,3,1,0:T(1,128)S(1)}, f32[2,3,1,6,4096]{4,2,3,1,0:T(1,128)S(1)}, u32[]{:S(2)}, u32[]{:S(2)}) collective-permute-start(f32[2,3,1,6,4096]{4,2,3,1,0:T(1,128)S(1)} %get-tuple-element.15), channel_id=1, source_target_pairs={{0,1},{1,2},{2,3},{3,4},{4,5},{5,6},{6,7},{7,8},{8,9},{9,10},{10,1... | collective-permute-start | bytes 1769480 | tf_op jit(solution)/shard_map/ppermute | solution.py:19
  17.9 20.9 %collective-permute-start.1 = (f32[2,3,1,6,4096]{4,2,3,1,0:T(1,128)S(1)}, f32[2,3,1,6,4096]{4,2,3,1,0:T(1,128)S(1)}, u32[]{:S(2)}, u32[]{:S(2)}) collective-permute-start(f32[2,3,1,6,4096]{4,2,3,1,0:T(1,128)S(1)} %get-tuple-element.16), channel_id=1, source_target_pairs={{1,0},{2,1},{3,2},{4,3},{5,4},{6,5},{7,6},{8,7},{9,8},{10,9},{11,1... | collective-permute-start | bytes 1769480 | tf_op jit(solution)/shard_map/ppermute | solution.py:20
  54.3 4.1 %copy-start.1 = (f32[2,9,6,4096]{3,1,2,0:T(8,128)}, f32[2,9,6,4096]{3,1,2,0:T(8,128)S(1)}, u32[]{:S(2)}) copy-start(f32[2,9,6,4096]{3,1,2,0:T(8,128)S(1)} %get-tuple-element.28) | copy-start | bytes 5308420
  58.4 11.7 %slice-start = ((s8[4718592]{0:T(1024)(128)(4,1)}), s8[4194304]{0:T(1024)(128)(4,1)S(1)}, s32[]{:S(2)}) async-start(s8[4718592]{0:T(1024)(128)(4,1)} %bitcast.42), calls=%async_computation.1 | async-start | bytes 8388608
  61.5 8.7 %slice-start.1 = ((s8[4718592]{0:T(1024)(128)(4,1)}), s8[524288]{0:T(1024)(128)(4,1)S(1)}, s32[]{:S(2)}) async-start(s8[4718592]{0:T(1024)(128)(4,1)} %bitcast.42), calls=%async_computation.2 | async-start | bytes 1048576
  70.1 4.3 %copy-start.3 = (f32[2,1,8,6,4096]{4,2,3,0,1:T(8,128)}, f32[2,1,8,6,4096]{4,2,3,0,1:T(8,128)S(1)}, u32[]{:S(2)}) copy-start(f32[2,1,8,6,4096]{4,2,3,0,1:T(8,128)S(1)} %get-tuple-element.23) | copy-start | bytes 4718596
  70.2 13.8 %copy-start.7 = (s32[1,256]{1,0:T(1,128)S(1)}, s32[1,256]{1,0:T(1,128)}, u32[]{:S(2)}) copy-start(s32[1,256]{1,0:T(1,128)} %param.7) | copy-start | bytes 3076
  74.4 2.2 copy-start
  77.9 15.8 %collective-permute-start.2 = (f32[2,3,1,6,4096]{4,2,3,1,0:T(1,128)S(1)}, f32[2,3,1,6,4096]{4,2,3,1,0:T(1,128)S(1)}, u32[]{:S(2)}, u32[]{:S(2)}) collective-permute-start(f32[2,3,1,6,4096]{4,2,3,1,0:T(1,128)S(1)} %get-tuple-element.13), channel_id=1, source_target_pairs={{0,1},{1,2},{2,3},{3,4},{4,5},{5,6},{6,7},{7,8},{8,9},{9,10},{10,1... | collective-permute-start | bytes 1769480 | tf_op jit(solution)/shard_map/ppermute | solution.py:19
  79.9 20.1 %collective-permute-start.3 = (f32[2,3,1,6,4096]{4,2,3,1,0:T(1,128)S(1)}, f32[2,3,1,6,4096]{4,2,3,1,0:T(1,128)}, u32[]{:S(2)}, u32[]{:S(2)}) collective-permute-start(f32[2,3,1,6,4096]{4,2,3,1,0:T(1,128)S(1)} %get-tuple-element.14), channel_id=1, source_target_pairs={{1,0},{2,1},{3,2},{4,3},{5,4},{6,5},{7,6},{8,7},{9,8},{10,9},{11,1... | collective-permute-start | bytes 1769480 | tf_op jit(solution)/shard_map/ppermute | solution.py:20
  93.7 0.8 copy-start.6
  117.2 4.1 %copy-start.2 = (f32[2,9,6,4096]{3,1,2,0:T(8,128)}, f32[2,9,6,4096]{3,1,2,0:T(8,128)S(1)}, u32[]{:S(2)}) copy-start(f32[2,9,6,4096]{3,1,2,0:T(8,128)S(1)} %get-tuple-element.22) | copy-start | bytes 5308420
  121.3 12.3 %slice-start.2 = ((s8[4718592]{0:T(1024)(128)(4,1)}), s8[4194304]{0:T(1024)(128)(4,1)S(1)}, s32[]{:S(2)}) async-start(s8[4718592]{0:T(1024)(128)(4,1)} %bitcast.45), calls=%async_computation.3 | async-start | bytes 8388608
  124.4 9.3 %slice-start.3 = ((s8[4718592]{0:T(1024)(128)(4,1)}), s8[524288]{0:T(1024)(128)(4,1)S(1)}, s32[]{:S(2)}) async-start(s8[4718592]{0:T(1024)(128)(4,1)} %bitcast.45), calls=%async_computation.4 | async-start | bytes 1048576
  124.4 9.3 %copy-start.4 = (f32[2,1,8,6,4096]{4,2,3,0,1:T(8,128)S(1)}, f32[2,1,8,6,4096]{4,2,3,0,1:T(8,128)}, u32[]{:S(2)}) copy-start(f32[2,1,8,6,4096]{4,2,3,0,1:T(8,128)} %copy-done.3) | copy-start | bytes 4718596
  215.2 5.9 %collective-permute-start.4 = (f32[2,4096]{1,0:T(2,128)S(1)}, f32[2,4096]{1,0:T(2,128)S(1)}, u32[]{:S(2)}, u32[]{:S(2)}) collective-permute-start(f32[2,4096]{1,0:T(2,128)S(1)} %get-tuple-element.29), channel_id=1, source_target_pairs={{0,1},{1,2},{2,3},{3,4},{4,5},{5,6},{6,7},{7,8},{8,9},{9,10},{10,1... | collective-permute-start | bytes 98312 | tf_op jit(solution)/shard_map/ppermute | solution.py:19
  217.7 10.0 %collective-permute-start.5 = (f32[2,4096]{1,0:T(2,128)S(1)}, f32[2,4096]{1,0:T(2,128)S(1)}, u32[]{:S(2)}, u32[]{:S(2)}) collective-permute-start(f32[2,4096]{1,0:T(2,128)S(1)} %get-tuple-element.30), channel_id=1, source_target_pairs={{1,0},{2,1},{3,2},{4,3},{5,4},{6,5},{7,6},{8,7},{9,8},{10,9},{11,1... | collective-permute-start | bytes 98312 | tf_op jit(solution)/shard_map/ppermute | solution.py:20
Sparse Core Ops, SparseCore 0:
  140.2 73.3 all-reduce.18
where the time goes:
time: 237 us; the launch traced here: 236 us
  waiting for transfers between devices  114 us (48%)
  other arithmetic  52.8 us (22%)
  local copies, waits for them, and re-layouts  37.7 us (16%)
  starting transfers between devices  17.7 us (7%)
  between operations  14.3 us (6%)
    psum x1, waiting for transfers between devices, on_device(): row_sum = lax.psum(density, 'wave')  73.5 us
    ppermute x3, waiting for transfers between devices, padded_2(): before = lax.ppermute(last, axis, up)  20.8 us
    ppermute x3, waiting for transfers between devices, padded_2(): after = lax.ppermute(initial, axis, down)  19.4 us
    another operation x2, other arithmetic, curl_curl(): return jnp.stack([curl_x, curl_y, curl_z], -4)  17.9 us
    sub x2, other arithmetic, curl_curl(): mag_z = ahead_x(comp_y) - ahead_y(lead_x)  11.5 us
    ppermute x3, starting transfers between devices, padded_2(): after = lax.ppermute(initial, axis, down)  9.93 us
    add x2, other arithmetic, relax_step(): fields + RELAX * (drive_all - curl_curl(padded) - wave_sq * permit * fiel...  9.77 us
    slice x4, local copies, waits for them, and re-layouts, behind_z(): values[..., :-1, :]  8.64 us
  transfers between devices with their start and end apart: 7, of which 6 were waited for; matrix products, arithmetic and copies ran while one was open for 0% of the time, Pallas kernels for 0%

commit v1 on v0

--- a/solution.py
+++ b/solution.py
@@ -87,7 +87,7 @@
         padded = padded_2(fields, (("brick", 2),), 1)
         fields = relax_step(fields, padded, drive_all, permittivity, wave_sq, diagonal)
     density = -wave_sq * jnp.sum(fields[0] * fields[1], axis=(0, 2))
-    row_sum = lax.psum(density, "wave")
+    row_sum = jnp.sum(lax.all_gather(density, "wave"), axis=0)
     along_y = smooth_padded(jnp.pad(row_sum, ((0, 0), (RADIUS, RADIUS))), columns, 1)
     widened_rows = padded_2(along_y, (("brick", 0),), RADIUS)
     smooth = smooth_padded(widened_rows, brick_rows, 0)

time: 237 us -> 194 us (0.82)
  waiting for transfers between devices: 114 us -> 71.4 us
    psum x1 -> x0, waiting for transfers between devices: 73.5 us -> none  [on_device(): row_sum = lax.psum(density, 'wave')]
    all_gather x0 -> x1, waiting for transfers between devices: none -> 30.7 us  [on_device(): row_sum = jnp.sum(lax.all_gather(density, 'wave'), axis=0)]
where the time goes in v1:
time: 194 us
  waiting for transfers between devices  71.4 us (37%)
  other arithmetic  52.7 us (27%)
  local copies, waits for them, and re-layouts  37.7 us (19%)
  starting transfers between devices  17.7 us (9%)
  between operations  14.3 us (7%)
    all_gather x1, waiting for transfers between devices, on_device(): row_sum = jnp.sum(lax.all_gather(density, 'wave'), axis=0)  30.7 us
    ppermute x3, waiting for transfers between devices, padded_2(): before = lax.ppermute(last, axis, up)  20.8 us
    ppermute x3, waiting for transfers between devices, padded_2(): after = lax.ppermute(initial, axis, down)  19.8 us
    another operation x2, other arithmetic, curl_curl(): return jnp.stack([curl_x, curl_y, curl_z], -4)  17.9 us
    sub x2, other arithmetic, curl_curl(): mag_z = ahead_x(comp_y) - ahead_y(lead_x)  11.5 us
    add x2, other arithmetic, relax_step(): fields + RELAX * (drive_all - curl_curl(padded) - wave_sq * permit * fiel...  9.76 us
    ppermute x3, starting transfers between devices, padded_2(): after = lax.ppermute(initial, axis, down)  9.47 us
    slice x4, local copies, waits for them, and re-layouts, behind_z(): values[..., :-1, :]  8.64 us
  transfers between devices with their start and end apart: 7, of which 6 were waited for; matrix products, arithmetic and copies ran while one was open for 0% of the time, Pallas kernels for 0%

profile of v1, /device:TPU:30, one launch (start us, length us, event | category | flops | bytes accessed | tf_op | source)
XLA Modules:
  0.0 193.8 jit_solution(15582382261910611283)
XLA Ops:
  10.3 3.0 %multiply_divide_fusion = f32[2,3,8,6,4096]{4,2,3,1,0:T(8,128)S(1)} fusion(f32[2,3,8,6,4096]{4,2,3,1,0:T(8,128)} %bitcast.43, f32[8,6,4096]{2,0,1:T(8,128)S(1)} %get-tuple-element.5), kind=kLoop, calls=%fused_computation.14 | loop fusion | flops 2359296 | bytes 10223616 | tf_op jit(solution)/shard_map/div | solution.py:85
  14.5 3.4 %collective-permute-start = (f32[2,3,1,6,4096]{4,2,3,1,0:T(1,128)S(1)}, f32[2,3,1,6,4096]{4,2,3,1,0:T(1,128)S(1)}, u32[]{:S(2)}, u32[]{:S(2)}) collective-permute-start(f32[2,3,1,6,4096]{4,2,3,1,0:T(1,128)S(1)} %get-tuple-element.15), channel_id=1, source_target_pairs={{0,1},{1,2},{2,3},{3,4},{4,5},{5,6},{6,7},{7,8},{8,9},{9,10},{10,1... | collective-permute-start | bytes 1769480 | tf_op jit(solution)/shard_map/ppermute | solution.py:19
  17.9 2.4 %collective-permute-start.1 = (f32[2,3,1,6,4096]{4,2,3,1,0:T(1,128)S(1)}, f32[2,3,1,6,4096]{4,2,3,1,0:T(1,128)S(1)}, u32[]{:S(2)}, u32[]{:S(2)}) collective-permute-start(f32[2,3,1,6,4096]{4,2,3,1,0:T(1,128)S(1)} %get-tuple-element.16), channel_id=1, source_target_pairs={{1,0},{2,1},{3,2},{4,3},{5,4},{6,5},{7,6},{8,7},{9,8},{10,9},{11,1... | collective-permute-start | bytes 1769480 | tf_op jit(solution)/shard_map/ppermute | solution.py:20
  20.3 11.1 %collective-permute-done = f32[2,3,1,6,4096]{4,2,3,1,0:T(1,128)S(1)} collective-permute-done((f32[2,3,1,6,4096]{4,2,3,1,0:T(1,128)S(1)}, f32[2,3,1,6,4096]{4,2,3,1,0:T(1,128)S(1)}, u32[]{:S(2)}, u32[]{:S(2)}) %collective-permute-start) | collective-permute-done | bytes 589856 | tf_op jit(solution)/shard_map/ppermute | solution.py:19
  31.4 7.3 %collective-permute-done.1 = f32[2,3,1,6,4096]{4,2,3,1,0:T(1,128)S(1)} collective-permute-done((f32[2,3,1,6,4096]{4,2,3,1,0:T(1,128)S(1)}, f32[2,3,1,6,4096]{4,2,3,1,0:T(1,128)S(1)}, u32[]{:S(2)}, u32[]{:S(2)}) %collective-permute-start.1) | collective-permute-done | bytes 589856 | tf_op jit(solution)/shard_map/ppermute | solution.py:20
  44.3 2.6 %slice.281 = f32[2,9,6,4095]{3,1,2,0:T(8,128)} slice(f32[2,10,6,4096]{3,1,2,0:T(8,128)S(1)} %get-tuple-element.11), slice={[0:2], [0:9], [0:6], [1:4096]} | slice | bytes 3538080 | tf_op jit(solution)/shard_map/slice | solution.py:30
  48.6 5.7 %fusion.10 = (f32[2,9,6,4096]{3,1,2,0:T(8,128)S(1)}, f32[2,9,6,4096]{3,1,2,0:T(8,128)}, f32[2,9,6,4096]{3,1,2,0:T(8,128)S(1)}) fusion(f32[2,10,6,4096]{3,1,2,0:T(8,128)S(1)} %get-tuple-element.10, f32[2,9,6,4095]{3,1,2,0:T(8,128)S(1)} %slice.271, f32[2,10,6,4096]{3,1,2,0:T(8,128)S(1)} %get-tuple-element.12, f32[2,10,6,4096]{3,1,2,0:T(8,128)S(1)} %get-tuple-element.11, ...), kind=kLoop, calls=%fused_computation.27 | loop fusion | flops 3981312 | bytes 20642976 | tf_op jit(solution)/shard_map/sub | solution.py:54
  58.4 3.1 %slice.280 = f32[2,8,5,4096]{3,1,2,0:T(8,128)} slice(f32[2,9,6,4096]{3,1,2,0:T(8,128)} %get-tuple-element.27), slice={[0:2], [1:9], [0:5], [0:4096]} | slice | bytes 2621440 | tf_op jit(solution)/shard_map/slice | solution.py:42
  61.5 8.6 %subtract_bitcast_fusion.1 = (f32[2,1,8,6,4096]{4,2,3,0,1:T(8,128)S(1)}, f32[2,1,8,6,4096]{4,2,3,0,1:T(8,128)}, f32[2,1,8,6,4096]{4,2,3,0,1:T(8,128)}) fusion(f32[2,8,5,4096]{3,1,2,0:T(8,128)} %slice.280, f32[2,8,6,4095]{3,1,2,0:T(8,128)} %slice.274, f32[2,9,6,4096]{3,1,2,0:T(8,128)} %get-tuple-element.27, f32[2,9,6,4096]{3,1,2,0:T(8,128)S(1)} %get-tuple-element.26, ...), kind=kLoop, calls=%fused_computation.46 | loop fusion | flops 3538944 | bytes 18349312 | tf_op jit(solution)/shard_map/stack | solution.py:58
  70.2 4.3 %fusion.6 = f32[2,3,8,6,4096]{4,2,3,1,0:T(8,128)S(1)} fusion(f32[8,6,4096]{2,0,1:T(8,128)} %get-tuple-element.6, f32[8,6,4096]{2,0,1:T(8,128)} %copy-done.5, f32[2,3,8,6,4096]{4,2,3,1,0:T(8,128)S(1)} %bitcast.46, f32[2,1,8,6,4096]{4,2,3,0,1:T(8,128)} %get-tuple-element.25, f32[2,1,8,6,4096]{4,2,3,0,1:T(8,128)} %get-tuple-element.24, ...), kind=kLoop, calls=%fused_computation.13 | loop fusion | flops 11796480 | bytes 15728640 | tf_op jit(solution)/shard_map/add | solution.py:62
  74.4 2.2 %copy-done = f32[2,3,8,6,4096]{4,2,3,1,0:T(8,128)} copy-done((f32[2,3,8,6,4096]{4,2,3,1,0:T(8,128)}, f32[2,3,8,6,4096]{4,2,3,1,0:T(8,128)S(1)}, u32[]{:S(2)}) %copy-start) | copy-done | bytes 4718616
  79.9 4.1 %collective-permute-start.3 = (f32[2,3,1,6,4096]{4,2,3,1,0:T(1,128)S(1)}, f32[2,3,1,6,4096]{4,2,3,1,0:T(1,128)}, u32[]{:S(2)}, u32[]{:S(2)}) collective-permute-start(f32[2,3,1,6,4096]{4,2,3,1,0:T(1,128)S(1)} %get-tuple-element.14), channel_id=1, source_target_pairs={{1,0},{2,1},{3,2},{4,3},{5,4},{6,5},{7,6},{8,7},{9,8},{10,9},{11,1... | collective-permute-start | bytes 1769480 | tf_op jit(solution)/shard_map/ppermute | solution.py:20
  84.0 9.7 %collective-permute-done.2 = f32[2,3,1,6,4096]{4,2,3,1,0:T(1,128)S(1)} collective-permute-done((f32[2,3,1,6,4096]{4,2,3,1,0:T(1,128)S(1)}, f32[2,3,1,6,4096]{4,2,3,1,0:T(1,128)S(1)}, u32[]{:S(2)}, u32[]{:S(2)}) %collective-permute-start.2) | collective-permute-done | bytes 589856 | tf_op jit(solution)/shard_map/ppermute | solution.py:19
  94.5 5.4 %collective-permute-done.3 = f32[2,3,1,6,4096]{4,2,3,1,0:T(1,128)} collective-permute-done((f32[2,3,1,6,4096]{4,2,3,1,0:T(1,128)S(1)}, f32[2,3,1,6,4096]{4,2,3,1,0:T(1,128)}, u32[]{:S(2)}, u32[]{:S(2)}) %collective-permute-start.3) | collective-permute-done | bytes 589856 | tf_op jit(solution)/shard_map/ppermute | solution.py:20
  100.0 3.5 %pad_maximum_fusion.1 = f32[2,3,10,6,4096]{4,2,3,1,0:T(8,128)S(1)} fusion(f32[2,3,1,6,4096]{4,2,3,1,0:T(1,128)} %collective-permute-done.3, f32[2,3,8,6,4096]{4,2,3,1,0:T(8,128)} %copy-done, f32[2,3,1,6,4096]{4,2,3,1,0:T(1,128)} %copy-done.6), kind=kLoop, calls=%fused_computation.2 | loop fusion | flops 2949120 | bytes 11796480 | tf_op jit(solution)/shard_map/concatenate | solution.py:21
  107.1 2.6 %slice.304 = f32[2,9,6,4095]{3,1,2,0:T(8,128)} slice(f32[2,10,6,4096]{3,1,2,0:T(8,128)S(1)} %get-tuple-element.8), slice={[0:2], [0:9], [0:6], [1:4096]} | slice | bytes 3538080 | tf_op jit(solution)/shard_map/slice | solution.py:30
  111.4 5.7 %fusion.8 = (f32[2,9,6,4096]{3,1,2,0:T(8,128)S(1)}, f32[2,9,6,4096]{3,1,2,0:T(8,128)}, f32[2,9,6,4096]{3,1,2,0:T(8,128)S(1)}) fusion(f32[2,10,6,4096]{3,1,2,0:T(8,128)S(1)} %get-tuple-element.7, f32[2,9,6,4095]{3,1,2,0:T(8,128)S(1)} %slice.294, f32[2,10,6,4096]{3,1,2,0:T(8,128)S(1)} %get-tuple-element.9, f32[2,10,6,4096]{3,1,2,0:T(8,128)S(1)} %get-tuple-element.8, ...), kind=kLoop, calls=%fused_computation.20 | loop fusion | flops 3981312 | bytes 20642976 | tf_op jit(solution)/shard_map/sub | solution.py:54
  121.3 3.1 %slice.303 = f32[2,8,5,4096]{3,1,2,0:T(8,128)} slice(f32[2,9,6,4096]{3,1,2,0:T(8,128)} %get-tuple-element.21), slice={[0:2], [1:9], [0:5], [0:4096]} | slice | bytes 2621440 | tf_op jit(solution)/shard_map/slice | solution.py:42
  124.4 9.2 %subtract_bitcast_fusion = (f32[2,1,8,6,4096]{4,2,3,0,1:T(8,128)}, f32[2,1,8,6,4096]{4,2,3,0,1:T(8,128)}, f32[2,1,8,6,4096]{4,2,3,0,1:T(8,128)}) fusion(f32[2,8,5,4096]{3,1,2,0:T(8,128)} %slice.303, f32[2,8,6,4095]{3,1,2,0:T(8,128)} %slice.297, f32[2,9,6,4096]{3,1,2,0:T(8,128)} %get-tuple-element.21, f32[2,9,6,4096]{3,1,2,0:T(8,128)S(1)} %get-tuple-element.20, ...), kind=kLoop, calls=%fused_computation.45 | loop fusion | flops 3538944 | bytes 18349312 | tf_op jit(solution)/shard_map/stack | solution.py:58
  133.6 5.5 %fusion.3 = f32[2,3,8,6,4096]{4,2,3,1,0:T(8,128)S(1)} fusion(f32[2,3,8,6,4096]{4,2,3,1,0:T(8,128)S(1)} %bitcast.49, f32[8,6,4096]{2,0,1:T(8,128)} %get-tuple-element.6, f32[8,6,4096]{2,0,1:T(8,128)} %copy-done.5, f32[2,1,8,6,4096]{4,2,3,0,1:T(8,128)} %get-tuple-element.19, f32[2,1,8,6,4096]{4,2,3,0,1:T(8,128)} %get-tuple-element.18, ...), kind=kLoop, calls=%fused_computation.9 | loop fusion | flops 21233664 | bytes 20447232 | tf_op jit(solution)/shard_map/add | solution.py:62
  140.1 30.7 %all-gather.3.cloned.1.call-done = f32[64,4096]{1,0:T(8,128)} async-done(((f32[8,4096]{1,0:T(8,128)}), f32[64,4096]{1,0:T(8,128)}) %all-gather.3.cloned.1.call-update) | async-done | bytes 1048592 | tf_op jit(solution)/shard_map/all_gather | solution.py:90
  172.3 2.9 %collective-permute-start.4 = (f32[2,4096]{1,0:T(2,128)S(1)}, f32[2,4096]{1,0:T(2,128)S(1)}, u32[]{:S(2)}, u32[]{:S(2)}) collective-permute-start(f32[2,4096]{1,0:T(2,128)S(1)} %get-tuple-element.29), channel_id=1, source_target_pairs={{0,1},{1,2},{2,3},{3,4},{4,5},{5,6},{6,7},{7,8},{8,9},{9,10},{10,1... | collective-permute-start | bytes 98312 | tf_op jit(solution)/shard_map/ppermute | solution.py:19
  175.3 2.9 %collective-permute-start.5 = (f32[2,4096]{1,0:T(2,128)S(1)}, f32[2,4096]{1,0:T(2,128)S(1)}, u32[]{:S(2)}, u32[]{:S(2)}) collective-permute-start(f32[2,4096]{1,0:T(2,128)S(1)} %get-tuple-element.30), channel_id=1, source_target_pairs={{1,0},{2,1},{3,2},{4,3},{5,4},{6,5},{7,6},{8,7},{9,8},{10,9},{11,1... | collective-permute-start | bytes 98312 | tf_op jit(solution)/shard_map/ppermute | solution.py:20
  178.2 7.1 %collective-permute-done.5 = f32[2,4096]{1,0:T(2,128)S(1)} collective-permute-done((f32[2,4096]{1,0:T(2,128)S(1)}, f32[2,4096]{1,0:T(2,128)S(1)}, u32[]{:S(2)}, u32[]{:S(2)}) %collective-permute-start.5) | collective-permute-done | bytes 32800 | tf_op jit(solution)/shard_map/ppermute | solution.py:20
  (59 shorter events, 33.2 us)
Async XLA Ops:
  6.5 164.3 %all-gather.3.cloned.1.call-start = ((), (), s32[]{:S(2)}) async-start(), calls=%async_computation | async-start | bytes 1179648 | tf_op jit(solution)/shard_map/all_gather | solution.py:90
  9.3 0.9 copy-start.5
  14.5 17.0 %collective-permute-start = (f32[2,3,1,6,4096]{4,2,3,1,0:T(1,128)S(1)}, f32[2,3,1,6,4096]{4,2,3,1,0:T(1,128)S(1)}, u32[]{:S(2)}, u32[]{:S(2)}) collective-permute-start(f32[2,3,1,6,4096]{4,2,3,1,0:T(1,128)S(1)} %get-tuple-element.15), channel_id=1, source_target_pairs={{0,1},{1,2},{2,3},{3,4},{4,5},{5,6},{6,7},{7,8},{8,9},{9,10},{10,1... | collective-permute-start | bytes 1769480 | tf_op jit(solution)/shard_map/ppermute | solution.py:19
  17.9 20.9 %collective-permute-start.1 = (f32[2,3,1,6,4096]{4,2,3,1,0:T(1,128)S(1)}, f32[2,3,1,6,4096]{4,2,3,1,0:T(1,128)S(1)}, u32[]{:S(2)}, u32[]{:S(2)}) collective-permute-start(f32[2,3,1,6,4096]{4,2,3,1,0:T(1,128)S(1)} %get-tuple-element.16), channel_id=1, source_target_pairs={{1,0},{2,1},{3,2},{4,3},{5,4},{6,5},{7,6},{8,7},{9,8},{10,9},{11,1... | collective-permute-start | bytes 1769480 | tf_op jit(solution)/shard_map/ppermute | solution.py:20
  54.3 4.1 %copy-start.1 = (f32[2,9,6,4096]{3,1,2,0:T(8,128)}, f32[2,9,6,4096]{3,1,2,0:T(8,128)S(1)}, u32[]{:S(2)}) copy-start(f32[2,9,6,4096]{3,1,2,0:T(8,128)S(1)} %get-tuple-element.28) | copy-start | bytes 5308420
  58.4 11.7 %slice-start = ((s8[4718592]{0:T(1024)(128)(4,1)}), s8[4194304]{0:T(1024)(128)(4,1)S(1)}, s32[]{:S(2)}) async-start(s8[4718592]{0:T(1024)(128)(4,1)} %bitcast.44), calls=%async_computation.1 | async-start | bytes 8388608
  61.5 8.7 %slice-start.1 = ((s8[4718592]{0:T(1024)(128)(4,1)}), s8[524288]{0:T(1024)(128)(4,1)S(1)}, s32[]{:S(2)}) async-start(s8[4718592]{0:T(1024)(128)(4,1)} %bitcast.44), calls=%async_computation.2 | async-start | bytes 1048576
  70.1 4.3 %copy-start.3 = (f32[2,1,8,6,4096]{4,2,3,0,1:T(8,128)}, f32[2,1,8,6,4096]{4,2,3,0,1:T(8,128)S(1)}, u32[]{:S(2)}) copy-start(f32[2,1,8,6,4096]{4,2,3,0,1:T(8,128)S(1)} %get-tuple-element.23) | copy-start | bytes 4718596
  74.4 2.2 %copy-start = (f32[2,3,8,6,4096]{4,2,3,1,0:T(8,128)}, f32[2,3,8,6,4096]{4,2,3,1,0:T(8,128)S(1)}, u32[]{:S(2)}) copy-start(f32[2,3,8,6,4096]{4,2,3,1,0:T(8,128)S(1)} %fusion.6) | copy-start | bytes 14155780
  77.9 15.8 %collective-permute-start.2 = (f32[2,3,1,6,4096]{4,2,3,1,0:T(1,128)S(1)}, f32[2,3,1,6,4096]{4,2,3,1,0:T(1,128)S(1)}, u32[]{:S(2)}, u32[]{:S(2)}) collective-permute-start(f32[2,3,1,6,4096]{4,2,3,1,0:T(1,128)S(1)} %get-tuple-element.13), channel_id=1, source_target_pairs={{0,1},{1,2},{2,3},{3,4},{4,5},{5,6},{6,7},{7,8},{8,9},{9,10},{10,1... | collective-permute-start | bytes 1769480 | tf_op jit(solution)/shard_map/ppermute | solution.py:19
  79.9 20.1 %collective-permute-start.3 = (f32[2,3,1,6,4096]{4,2,3,1,0:T(1,128)S(1)}, f32[2,3,1,6,4096]{4,2,3,1,0:T(1,128)}, u32[]{:S(2)}, u32[]{:S(2)}) collective-permute-start(f32[2,3,1,6,4096]{4,2,3,1,0:T(1,128)S(1)} %get-tuple-element.14), channel_id=1, source_target_pairs={{1,0},{2,1},{3,2},{4,3},{5,4},{6,5},{7,6},{8,7},{9,8},{10,9},{11,1... | collective-permute-start | bytes 1769480 | tf_op jit(solution)/shard_map/ppermute | solution.py:20
  93.7 0.8 copy-start.6
  117.2 4.1 %copy-start.2 = (f32[2,9,6,4096]{3,1,2,0:T(8,128)}, f32[2,9,6,4096]{3,1,2,0:T(8,128)S(1)}, u32[]{:S(2)}) copy-start(f32[2,9,6,4096]{3,1,2,0:T(8,128)S(1)} %get-tuple-element.22) | copy-start | bytes 5308420
  121.3 12.3 %slice-start.2 = ((s8[4718592]{0:T(1024)(128)(4,1)}), s8[4194304]{0:T(1024)(128)(4,1)S(1)}, s32[]{:S(2)}) async-start(s8[4718592]{0:T(1024)(128)(4,1)} %bitcast.47), calls=%async_computation.3 | async-start | bytes 8388608
  124.4 9.3 %slice-start.3 = ((s8[4718592]{0:T(1024)(128)(4,1)}), s8[524288]{0:T(1024)(128)(4,1)S(1)}, s32[]{:S(2)}) async-start(s8[4718592]{0:T(1024)(128)(4,1)} %bitcast.47), calls=%async_computation.4 | async-start | bytes 1048576
  124.4 9.3 %copy-start.4 = (f32[2,1,8,6,4096]{4,2,3,0,1:T(8,128)S(1)}, f32[2,1,8,6,4096]{4,2,3,0,1:T(8,128)}, u32[]{:S(2)}) copy-start(f32[2,1,8,6,4096]{4,2,3,0,1:T(8,128)} %copy-done.3) | copy-start | bytes 4718596
  139.1 0.9 copy-start.7
  172.3 5.9 %collective-permute-start.4 = (f32[2,4096]{1,0:T(2,128)S(1)}, f32[2,4096]{1,0:T(2,128)S(1)}, u32[]{:S(2)}, u32[]{:S(2)}) collective-permute-start(f32[2,4096]{1,0:T(2,128)S(1)} %get-tuple-element.29), channel_id=1, source_target_pairs={{0,1},{1,2},{2,3},{3,4},{4,5},{5,6},{6,7},{7,8},{8,9},{9,10},{10,1... | collective-permute-start | bytes 98312 | tf_op jit(solution)/shard_map/ppermute | solution.py:19
  175.3 10.0 %collective-permute-start.5 = (f32[2,4096]{1,0:T(2,128)S(1)}, f32[2,4096]{1,0:T(2,128)S(1)}, u32[]{:S(2)}, u32[]{:S(2)}) collective-permute-start(f32[2,4096]{1,0:T(2,128)S(1)} %get-tuple-element.30), channel_id=1, source_target_pairs={{1,0},{2,1},{3,2},{4,3},{5,4},{6,5},{7,6},{8,7},{9,8},{10,9},{11,1... | collective-permute-start | bytes 98312 | tf_op jit(solution)/shard_map/ppermute | solution.py:20
Sparse Core Ops, SparseCore 0:
  140.2 30.5 all-gather.2
